TPU v7x, 256 devices: a whole 4x4x8 slice. The times are simulated.
256 devices in a mesh: replica: 8 (over z_lo, y), tensor: 32 (over x, z_hi, core).
Axes of the slice: x: 4, y: 4, z: 8 (z_hi: 4, z_lo: 2; z = z_hi * 2 + z_lo), core: 2. Of those that a mesh axis runs over, the one named last changes fastest.
Arguments:
- activations: bfloat16 [65536, 832], P(('replica', 'tensor')), may hold values from -6 to 6
- out_grad: bfloat16 [65536, 14336], P('replica', 'tensor'), may hold values from -0.0625 to 0.0625
- master_weights: float32 [6656, 14336], P('replica', 'tensor'), may hold values from -6 to 6
- first_moment: float32 [6656, 14336], P('replica', 'tensor'), may hold values from -0.6 to 0.6
- second_moment: float32 [6656, 14336], P('replica', 'tensor'), may hold values from 0.01 to 1
- anchor: float32 [832, 14336], P(None, 'tensor'), may hold values from -6 to 6
- outer_momentum: float32 [832, 14336], P(None, 'tensor'), may hold values from -3 to 3
Outputs:
- rebuilt_weights: bfloat16 [832, 14336], P(None, 'tensor')
- new_momentum: float32 [832, 14336], P(None, 'tensor')
All inputs are finite; a program needn't handle non-finite values.
Results may differ from a plain program's by a relative error of at most 0.001.
Values may be sent and summed in bfloat16 or wider, within the bound.
A program may use at most 128 MiB of HBM per device.

v0:
```python
import jax
import jax.numpy as jnp
from jax import lax
from jax.sharding import PartitionSpec as P

BETA_ONE = 0.9
BETA_TWO = 0.95
BIAS_ONE = 0.9999734386
BIAS_TWO = 0.9940794708
EPSILON = 1e-08
INNER_RATE = 0.25
DECAY_RATE = 0.1
OUTER_RATE = 0.7
NESTEROV = 0.9


def split_up(x, dim, devices):
    before, after = (x.shape[:dim], x.shape[dim + 1 :])
    return jnp.moveaxis(x.reshape(*before, devices, -1, *after), dim, 0)


def sent_and_summed(x, axis, dim):
    devices = lax.axis_size(axis)
    pieces = lax.all_to_all(split_up(x, dim, devices), axis, 0, 0, tiled=True)
    return jnp.sum(pieces, axis=0)


def outer_update(pseudo_mean, anchor_rows, momentum_rows):
    new_momentum = NESTEROV * momentum_rows + pseudo_mean
    rebuilt = anchor_rows - OUTER_RATE * (pseudo_mean + NESTEROV * new_momentum)
    return (rebuilt.astype(jnp.bfloat16), new_momentum)


def on_device(
    activations, out_grad, master_weights, first_moment, second_moment, anchor, outer_momentum
):
    numbers = (((0,), (0,)), ((), ()))
    gathered = lax.all_gather(activations, "tensor", axis=0, tiled=True)
    gradient = lax.dot_general(gathered, out_grad, numbers, preferred_element_type=jnp.float32)
    moment_one = BETA_ONE * first_moment + (1.0 - BETA_ONE) * gradient
    moment_two = BETA_TWO * second_moment + (1.0 - BETA_TWO) * gradient * gradient
    step_size = moment_one / BIAS_ONE / (jnp.sqrt(moment_two / BIAS_TWO) + EPSILON)
    updated = master_weights - INNER_RATE * (step_size + DECAY_RATE * master_weights)
    pseudo = anchor - updated
    groups = lax.axis_size("replica")
    shared_sum = sent_and_summed(pseudo, "replica", 0)
    share_rows = shared_sum.shape[0]
    first_row = lax.axis_index("replica") * share_rows
    anchor_rows = lax.dynamic_slice_in_dim(anchor, first_row, share_rows, 0)
    momentum_rows = lax.dynamic_slice_in_dim(outer_momentum, first_row, share_rows, 0)
    rebuilt_rows, moment_rows = outer_update(shared_sum / groups, anchor_rows, momentum_rows)
    rebuilt, new_momentum = (
        lax.all_gather(rebuilt_rows.astype(jnp.float32), "replica", axis=0, tiled=True).astype(
            rebuilt_rows.dtype
        ),
        lax.all_gather(moment_rows, "replica", axis=0, tiled=True),
    )
    return (rebuilt, new_momentum)


def solution(mesh):
    placed = (
        P(("replica", "tensor"), None),
        P("replica", "tensor"),
        P("replica", "tensor"),
        P("replica", "tensor"),
        P("replica", "tensor"),
        P(None, "tensor"),
        P(None, "tensor"),
    )
    return jax.shard_map(
        on_device,
        mesh=mesh,
        in_specs=placed,
        out_specs=(P(None, "tensor"), P(None, "tensor")),
        check_vma=False,
    )
```

profile of v0, /device:TPU:1, one launch (start us, length us, event | category | flops | bytes accessed | tf_op | source)
XLA Modules:
  0.0 219.3 jit_solution(12854751552474514137)
XLA Ops:
  7.2 0.0 all-gather.3.cloned.1.call-start
  7.2 0.7 all-gather.3.cloned.1.call-update
  7.9 117.9 %all-gather.3.cloned.1.call-done = bf16[8192,832]{0,1:T(8,128)(2,1)} async-done(((bf16[256,832]{0,1:T(8,128)(2,1)}), bf16[8192,832]{0,1:T(8,128)(2,1)}) %all-gather.3.cloned.1.call-update) | async-done | bytes 13631504 | tf_op jit(solution)/shard_map/all_gather | solution.py:38
  125.8 18.0 %subtract_subtract_fusion = f32[832,448]{0,1:T(8,128)S(1)} fusion(f32[832,448]{0,1:T(8,128)} %param.12, f32[832,448]{0,1:T(8,128)} %param.9, f32[832,448]{0,1:T(8,128)} %param.11, f32[832,448]{0,1:T(8,128)} %param.10, bf16[8192,832]{0,1:T(8,128)(2,1)} %all-gather.3.cloned.1.call-done, bf16[8192,448]{0,1:T(8,128)(2,1)} %param.8), kind=kOutput, calls=%fused_computation.7 | convolution fusion | flops 6112870400 | bytes 28426240 | tf_op jit(solution)/shard_map/dot_general | solution.py:39
  143.8 1.8 copy.11
  145.6 4.0 %all-to-all-start = ((f32[8,104,448]{2,1,0:T(8,128)}), f32[8,104,448]{2,1,0:T(8,128)S(1)}, u32[]{:S(2)}, u32[]{:S(2)}) async-start(f32[8,104,448]{2,1,0:T(8,128)} %bitcast), calls=%async_computation | async-start | bytes 3407872 | tf_op jit(solution)/shard_map/all_to_all | solution.py:24
  149.6 0.0 all-gather.5.cloned.1.call-start
  149.6 1.4 constant_dynamic-slice_fusion
  151.0 0.1 copy.16
  151.1 0.1 copy.15
  151.3 20.3 %all-to-all-done = f32[8,104,448]{2,1,0:T(8,128)S(1)} async-done(((f32[8,104,448]{2,1,0:T(8,128)}), f32[8,104,448]{2,1,0:T(8,128)S(1)}, u32[]{:S(2)}, u32[]{:S(2)}) %all-to-all-start) | async-done | bytes 1490976 | tf_op jit(solution)/shard_map/all_to_all | solution.py:24
  171.6 0.2 reduce_sum.9
  171.7 0.7 multiply_add_fusion
  172.5 0.0 all-gather.5.cloned.1.call-update
  172.5 26.5 %all_gather.10 = bf16[832,448]{1,0:T(8,128)(2,1)S(1)} all-gather(bf16[104,448]{1,0:T(8,128)(2,1)S(1)} %get-tuple-element.5), channel_id=1, replica_groups=mesh['replica'=8,'tensor'=32] {'replica'}, dimensions={0}, use_global_device_ids=true | all-gather | bytes 838656 | tf_op jit(solution)/shard_map/all_gather | solution.py:53
  199.0 1.2 copy.13
  200.2 9.6 %all-gather.5.cloned.1.call-done = f32[832,448]{1,0:T(8,128)} async-done(((f32[104,448]{1,0:T(8,128)}), f32[832,448]{1,0:T(8,128)}) %all-gather.5.cloned.1.call-update) | async-done | bytes 1490960 | tf_op jit(solution)/shard_map/all_gather | solution.py:56
  209.9 2.6 %copy.14 = f32[832,448]{0,1:T(8,128)} copy(f32[832,448]{1,0:T(8,128)} %all-gather.5.cloned.1.call-done) | data formatting | bytes 2981888
Async XLA Ops:
  7.2 118.7 %all-gather.3.cloned.1.call-start = ((), (), s32[]{:S(2)}) async-start(), calls=%async_computation.1 | async-start | bytes 14057472 | tf_op jit(solution)/shard_map/all_gather | solution.py:38
  145.6 26.0 %all-to-all-start = ((f32[8,104,448]{2,1,0:T(8,128)}), f32[8,104,448]{2,1,0:T(8,128)S(1)}, u32[]{:S(2)}, u32[]{:S(2)}) async-start(f32[8,104,448]{2,1,0:T(8,128)} %bitcast), calls=%async_computation | async-start | bytes 3407872 | tf_op jit(solution)/shard_map/all_to_all | solution.py:24
  149.6 60.3 %all-gather.5.cloned.1.call-start = ((), (), s32[]{:S(2)}) async-start(), calls=%async_computation.2 | async-start | bytes 1916928 | tf_op jit(solution)/shard_map/all_gather | solution.py:56
Sparse Core Ops, SparseCore 0:
  10.4 115.3 all-gather.2
  172.6 37.1 all-gather.4
where the time goes:
time: 223 us; the launch traced here: 219 us
  waiting for transfers between devices  149 us (67%)
  blocking collectives  26.5 us (12%)
  matrix products  18 us (8%)
  between operations  14.1 us (6%)
  local copies, waits for them, and re-layouts  7.22 us (3%)
  starting transfers between devices  4.1 us (2%)
    all_gather x1, waiting for transfers between devices, on_device(): gathered = lax.all_gather(activations, 'tensor', axis=0, tiled=True)  118 us
    all_gather x1, blocking collectives, on_device(): lax.all_gather(rebuilt_rows.astype(jnp.float32), 'replica', axis=0, tiled...  26.5 us
    all_to_all x1, waiting for transfers between devices, sent_and_summed(): pieces = lax.all_to_all(split_up(x, dim, devices), axis, 0, 0, tiled=True)  20.3 us
    dot_general x1, matrix products, on_device(): lax.dot_general(gathered, out_grad, numbers, preferred_element_type=jnp.f...  18 us
    all_gather x1, waiting for transfers between devices, on_device(): lax.all_gather(moment_rows, 'replica', axis=0, tiled=True)  9.62 us
  transfers between devices with their start and end apart: 3, of which 3 were waited for; matrix products, arithmetic and copies ran while one was open for 1% of the time, Pallas kernels for 0%

commit v1 on v0

v1 whole, which is shorter than its diff:
```python
import heapq

import jax
import jax.numpy as jnp
from jax import lax
from jax.experimental import pallas as pl
from jax.experimental.pallas import tpu as pltpu
from jax.sharding import PartitionSpec as P

BETA_ONE = 0.9
BETA_TWO = 0.95
BIAS_ONE = 0.9999734386
BIAS_TWO = 0.9940794708
EPSILON = 1e-08
INNER_RATE = 0.25
DECAY_RATE = 0.1
OUTER_RATE = 0.7
NESTEROV = 0.9

MESH = pl.DeviceIdType.MESH
NX, NZ, NC = 4, 4, 2
RING = (0, -1, 1, 2)

SIZES = (384, 256, 192)
RATE = {"x": 45e3, "z": 22e3, "d": 200e3}
DELAY = {"x": 2.0, "z": 3.0, "d": 1.0}
MATMUL_US, UPDATE_US, EXCHANGE_US = 15.0, 4.0, 26.0


def transfers(p):
    moves = {
        ("zA", p, 1): ("z", (0, 0), "all", 1, (0, -1)),
        ("zA", p, -1): ("z", (0, 0), "all", -1, (0, 1)),
        ("zB", p, 1): ("z", (0, -1), "low", 1, (0, -2)),
        ("zB", p, -1): ("z", (0, 1), "high", -1, (0, 2)),
    }
    for dz in RING:
        moves["xA", p, 1, dz] = ("x", (0, dz), "all", 1, (-1, dz))
        moves["xA", p, -1, dz] = ("x", (0, dz), "all", -1, (1, dz))
        moves["xB", p, 1, dz] = ("x", (-1, dz), "low", 1, (-2, dz))
        moves["xB", p, -1, dz] = ("x", (1, dz), "high", -1, (2, dz))
        for dx in RING:
            moves["D", p, dx, dz] = ("d", (dx, dz), "all", 0, (dx, dz))
    return moves


def plan(sizes):
    phases = len(sizes)
    total = sum(sizes)
    moves = {}
    for p in range(phases):
        moves.update(transfers(p))
    rules = []

    def own_z(p):
        return [("zA", p, 1), ("zA", p, -1)] if p < phases else []

    def own_x(p):
        return [("xA", p, 1, 0), ("xA", p, -1, 0)] if p < phases else []

    for p in range(phases):
        rules.append(([("zA", p, 1)], [("zB", p, 1), ("xA", p, 1, -1), ("xA", p, -1, -1), ("D", p, 0, -1)]))
        rules.append(([("zA", p, -1)], [("zB", p, -1), ("xA", p, 1, 1), ("xA", p, -1, 1), ("D", p, 0, 1)] + own_z(p + 1) + own_x(p + 2)))
        rules.append(([("zB", p, 1), ("zB", p, -1)], [("xA", p, 1, 2), ("xA", p, -1, 2), ("D", p, 0, 2)]))
        for dz in RING:
            rules.append(([("xA", p, 1, dz)], [("xB", p, 1, dz), ("D", p, -1, dz)]))
            rules.append(([("xA", p, -1, dz)], [("xB", p, -1, dz), ("D", p, 1, dz)]))
            rules.append(([("xB", p, 1, dz), ("xB", p, -1, dz)], [("D", p, 2, dz)]))
    steps, arrivals, free, done = [], [], {}, set()
    clock = 0.0
    serial = 0

    def send(names):
        nonlocal serial
        for name in names:
            link, _, part, way, _ = moves[name]
            lane = (link, way)
            size = sizes[name[1]] * 512 * (1.0 if part == "all" else 0.5)
            begin = max(clock, free.get(lane, 0.0))
            free[lane] = begin + size / RATE[link]
            heapq.heappush(arrivals, (free[lane] + DELAY[link], serial, name))
            serial += 1
        steps.append(("send", tuple(names)))

    def exchange(name, p):
        nonlocal serial
        begin = max(clock, free.get("y", 0.0))
        free["y"] = begin + EXCHANGE_US * sizes[p] / total
        heapq.heappush(arrivals, (free["y"] + 3.0, serial, (name, p)))
        serial += 1

    send(own_z(0) + own_x(0))
    send([("D", p, 0, 0) for p in range(phases)])
    send(own_x(1))
    arrived = set()
    tasks = []
    for p in range(phases):
        for dx in RING:
            needs = {("D", p, dx, dz) for dz in RING}
            for dz in RING:
                for name, move in moves.items():
                    if name[0] != "D" and name[1] == p and move[4] in ((dx, dz), (dx - 4, dz), (dx, dz - 4)):
                        needs.add(name)
            tasks.append((("mm", p, dx), needs, MATMUL_US / 4 * sizes[p] / total))
        tasks.append((("update", p), {("mm", p, dx) for dx in RING}, UPDATE_US * sizes[p] / total))
        tasks.append((("reduce", p), {("RS", p)}, UPDATE_US / 8 * sizes[p] / total))
        tasks.append((("final", p), {("AG", p)}, UPDATE_US / 2 * sizes[p] / total))
    waited = set()
    while rules or tasks:
        while arrivals and arrivals[0][0] <= clock:
            arrived.add(heapq.heappop(arrivals)[2])
        rule = next((r for r in rules if set(r[0]) <= arrived), None)
        if rule:
            rules.remove(rule)
            for name in rule[0]:
                waited.add(name)
                steps.append(("wait", name))
            send(rule[1])
            continue
        ready = [t for t in tasks if t[1] <= (arrived | done)]
        if ready:
            rank = {"final": 3, "reduce": 0, "update": 1, "mm": 2}
            task = min(ready, key=lambda t: rank[t[0][0]])
            tasks.remove(task)
            for name in sorted(task[1] - waited - done, key=str):
                waited.add(name)
                steps.append(("wait", name))
            steps.append(task[0])
            clock += task[2]
            done.add(task[0])
            if task[0][0] == "update":
                exchange("RS", task[0][1])
            if task[0][0] == "reduce":
                exchange("AG", task[0][1])
            continue
        clock = arrivals[0][0]
    return steps, moves, clock


def make_kernel(sizes, features, hidden, tokens, replicas):
    steps, moves, _ = plan(sizes)
    starts = [sum(sizes[:p]) for p in range(len(sizes))]
    index = {name: i for i, name in enumerate(sorted(moves, key=str))}
    share = hidden // replicas

    def kernel(
        act, grad, w_hbm, m_hbm, v_hbm, an_hbm, mo_hbm, reb_ref, mom_ref,
        held, g_buf, w_buf, m_buf, v_buf, an_buf, mo_buf, acc, landed, mean,
        out_sem, in_sem, rs_out, rs_in, ag_out, ag_in, load_sem,
    ):
        me_r, me_t = lax.axis_index("replica"), lax.axis_index("tensor")
        core = lax.rem(me_t, NC)
        zh = lax.rem(me_t // NC, NZ)
        x = me_t // (NC * NZ)

        def slot(dx, dz, c):
            return (lax.rem(x + dx + NX, NX) * NZ + lax.rem(zh + dz + NZ, NZ)) * NC + c

        def device(dx, dz, c):
            return {"replica": me_r, "tensor": slot(dx, dz, c)}

        def peer(j):
            return lax.rem(me_r + j + replicas, replicas)

        loads = [
            pltpu.make_async_copy(src, dst, load_sem.at[i])
            for i, (src, dst) in enumerate(
                ((act, held.at[me_t]), (grad, g_buf), (w_hbm, w_buf), (m_hbm, m_buf), (v_hbm, v_buf), (an_hbm, an_buf), (mo_hbm, mo_buf))
            )
        ]
        for load in loads:
            load.start()

        barrier = pltpu.get_barrier_semaphore()
        friends = [device(0, 1, core), device(0, -1, core), device(1, 0, core), device(-1, 0, core), device(0, 0, 1 - core)]
        friends += [{"replica": peer(j), "tensor": me_t} for j in range(1, replicas)]
        for friend in friends:
            pl.semaphore_signal(barrier, inc=1, device_id=friend, device_id_type=MESH)
        pl.semaphore_wait(barrier, len(friends))

        def rows_of(name):
            p, part = name[1], moves[name][2]
            half = sizes[p] // 2
            begin = starts[p] + (half if part == "high" else 0)
            return pl.ds(begin, sizes[p] if part == "all" else half)

        def outgoing(name):
            link, source, _, way, _ = moves[name]
            rows = rows_of(name)
            there = slot(*source, core)
            target = {"x": device(way, 0, core), "z": device(0, way, core), "d": device(0, 0, 1 - core)}[link]
            src = act.at[rows] if source == (0, 0) else held.at[there, rows]
            return pltpu.make_async_remote_copy(
                src_ref=src,
                dst_ref=held.at[there, rows],
                send_sem=out_sem.at[index[name]],
                recv_sem=in_sem.at[index[name]],
                device_id=target,
                device_id_type=MESH,
            )

        def incoming(name):
            link, _, _, _, got = moves[name]
            place = held.at[slot(*got, 1 - core if link == "d" else core), rows_of(name)]
            return pltpu.make_async_remote_copy(
                src_ref=place,
                dst_ref=place,
                send_sem=out_sem.at[index[name]],
                recv_sem=in_sem.at[index[name]],
                device_id=device(0, 0, 1 - core),
                device_id_type=MESH,
            )

        def columns(p):
            return pl.ds(starts[p], sizes[p])

        def share_rows(r):
            return pl.ds(pl.multiple_of(r * share, 8), share)

        def scatter(p, j):
            return pltpu.make_async_remote_copy(
                src_ref=acc.at[share_rows(peer(j)), columns(p)],
                dst_ref=landed.at[j - 1, :, columns(p)],
                send_sem=rs_out.at[p, j - 1],
                recv_sem=rs_in.at[p, j - 1],
                device_id={"replica": peer(j), "tensor": me_t},
                device_id_type=MESH,
            )

        def spread(p, j, owner):
            return pltpu.make_async_remote_copy(
                src_ref=mean.at[share_rows(owner), columns(p)],
                dst_ref=mean.at[share_rows(owner), columns(p)],
                send_sem=ag_out.at[p, j - 1],
                recv_sem=ag_in.at[p, j - 1],
                device_id={"replica": peer(j), "tensor": me_t},
                device_id_type=MESH,
            )

        def matmul(p, dx, first):
            base = lax.rem(x + dx + NX, NX) * (NZ * NC)
            cols = columns(p)

            def product(i):
                block = base + i
                left = g_buf[:, pl.ds(pl.multiple_of(block * tokens, tokens), tokens)]
                return lax.dot_general(left, held[block, cols, :], (((1,), (1,)), ((), ())), preferred_element_type=jnp.float32)

            if first:
                acc[:, cols] = product(0) + product(1)

            @pl.loop(1 if first else 0, NZ * NC // 2)
            def _(i):
                acc[:, cols] += product(2 * i) + product(2 * i + 1)

        def update(p):
            cols = columns(p)
            step = 32

            @pl.loop(0, hidden // step)
            def _(i):
                rows = pl.ds(pl.multiple_of(i * step, step), step)
                gradient = acc[rows, cols]
                weights = w_buf[rows, cols]
                moment_one = BETA_ONE * m_buf[rows, cols] + (1.0 - BETA_ONE) * gradient
                moment_two = BETA_TWO * v_buf[rows, cols] + (1.0 - BETA_TWO) * gradient * gradient
                size = moment_one * (1.0 / BIAS_ONE) / (jnp.sqrt(moment_two * (1.0 / BIAS_TWO)) + EPSILON)
                updated = weights - INNER_RATE * (size + DECAY_RATE * weights)
                acc[rows, cols] = an_buf[rows, cols] - updated

        def reduce(p):
            cols = columns(p)
            rows = share_rows(me_r)
            total = acc[rows, cols]
            for j in range(1, replicas):
                total = total + landed[j - 1, :, cols]
            mean[rows, cols] = total * (1.0 / replicas)

        def final(p):
            cols = columns(p)
            step = 32

            @pl.loop(0, hidden // step)
            def _(i):
                rows = pl.ds(pl.multiple_of(i * step, step), step)
                pseudo_mean = mean[rows, cols]
                new_momentum = NESTEROV * mo_buf[rows, cols] + pseudo_mean
                mom_ref[rows, cols] = new_momentum
                rebuilt = an_buf[rows, cols] - OUTER_RATE * (pseudo_mean + NESTEROV * new_momentum)
                reb_ref[rows, cols] = rebuilt.astype(reb_ref.dtype)

        multiplied, loaded = set(), set()

        def load_wait(*which):
            for i in which:
                if i not in loaded:
                    loaded.add(i)
                    loads[i].wait()

        for kind, *rest in steps:
            if kind == "send":
                for name in rest[0]:
                    outgoing(name).start()
            elif kind == "wait":
                name = rest[0]
                if name[0] == "RS":
                    for j in range(1, replicas):
                        scatter(name[1], j).wait_recv()
                elif name[0] == "AG":
                    for j in range(1, replicas):
                        spread(name[1], j, peer(-j)).wait_recv()
                else:
                    incoming(name).wait_recv()
            elif kind == "mm":
                load_wait(0, 1)
                p, dx = rest
                matmul(p, dx, p not in multiplied)
                multiplied.add(p)
            elif kind == "update":
                load_wait(2, 3, 4, 5)
                update(rest[0])
                for j in range(1, replicas):
                    scatter(rest[0], j).start()
            elif kind == "reduce":
                reduce(rest[0])
                for j in range(1, replicas):
                    spread(rest[0], j, me_r).start()
            elif kind == "final":
                load_wait(6)
                final(rest[0])
        for name in index:
            outgoing(name).wait_send()
        for p in range(len(sizes)):
            for j in range(1, replicas):
                scatter(p, j).wait_send()
                spread(p, j, me_r).wait_send()

    count = len(index)
    full = (hidden, features)
    scratch = [
        pltpu.VMEM((NX * NZ * NC, features, tokens), jnp.bfloat16),
        pltpu.VMEM((hidden, NX * NZ * NC * tokens), jnp.bfloat16),
        *[pltpu.VMEM(full, jnp.float32)] * 5,
        pltpu.VMEM(full, jnp.float32),
        pltpu.VMEM((replicas - 1, share, features), jnp.float32),
        pltpu.VMEM(full, jnp.float32),
        pltpu.SemaphoreType.DMA((count,)),
        pltpu.SemaphoreType.DMA((count,)),
        *[pltpu.SemaphoreType.DMA((len(sizes), replicas - 1))] * 4,
        pltpu.SemaphoreType.DMA((7,)),
    ]
    return kernel, scratch


def on_device(activations, out_grad, master_weights, first_moment, second_moment, anchor, outer_momentum):
    tokens, features = activations.shape
    hidden = out_grad.shape[1]
    replicas = lax.axis_size("replica")
    kernel, scratch = make_kernel(SIZES, features, hidden, tokens, replicas)
    rebuilt, momentum = pl.pallas_call(
        kernel,
        out_shape=(
            jax.ShapeDtypeStruct((hidden, features), jnp.bfloat16),
            jax.ShapeDtypeStruct((hidden, features), jnp.float32),
        ),
        in_specs=[pl.BlockSpec(memory_space=pl.ANY)] * 7,
        out_specs=(pl.BlockSpec(memory_space=pltpu.VMEM),) * 2,
        scratch_shapes=scratch,
        compiler_params=pltpu.CompilerParams(collective_id=0, has_side_effects=True, vmem_limit_bytes=60 * 2**20),
        name="diloco",
    )(*(a.T for a in (activations, out_grad, master_weights, first_moment, second_moment, anchor, outer_momentum)))
    return rebuilt.T, momentum.T


def solution(mesh):
    placed = (
        P(("replica", "tensor"), None),
        P("replica", "tensor"),
        P("replica", "tensor"),
        P("replica", "tensor"),
        P("replica", "tensor"),
        P(None, "tensor"),
        P(None, "tensor"),
    )
    return jax.shard_map(
        on_device,
        mesh=mesh,
        in_specs=placed,
        out_specs=(P(None, "tensor"), P(None, "tensor")),
        check_vma=False,
    )
```

time: 223 us -> 109 us (0.49); the launches traced: 219 us -> 109 us
  waiting for transfers between devices: 149 us -> 0 us
  Pallas kernels: 0 us -> 105 us
  blocking collectives: 26.5 us -> 0 us
  matrix products: 18 us -> 0 us
  between operations: 14.1 us -> 0.65 us
  starting transfers between devices: 4.1 us -> 0 us
  local copies, waits for them, and re-layouts: 7.22 us -> 3.36 us
    all_gather x2 -> x0, waiting for transfers between devices: 128 us -> none  [the longest x1 118 us: on_device(): gathered = lax.all_gather(activations, 'tensor', axis=0, tiled=True)]
    pallas_call x0 -> x1, Pallas kernels: none -> 105 us  [on_device(): pl.pallas_call(kernel, out_shape=(jax.ShapeDtypeStruct((hidden, features)...]
    all_gather x1 -> x0, blocking collectives: 26.5 us -> none  [on_device(): lax.all_gather(rebuilt_rows.astype(jnp.float32), 'replica', axis=0, tiled...]
    all_to_all x1 -> x0, waiting for transfers between devices: 20.3 us -> none  [sent_and_summed(): pieces = lax.all_to_all(split_up(x, dim, devices), axis, 0, 0, tiled=True)]
    dot_general x1 -> x0, matrix products: 18 us -> none  [on_device(): lax.dot_general(gathered, out_grad, numbers, preferred_element_type=jnp.f...]
    all_to_all x1 -> x0, starting transfers between devices: 4.02 us -> none  [sent_and_summed(): pieces = lax.all_to_all(split_up(x, dim, devices), axis, 0, 0, tiled=True)]
  transfers between devices with their start and end apart: 3 -> 0, of which waited for: 3 -> 0; matrix products, arithmetic and copies ran while one was open for 1% -> 0% of each run, Pallas kernels for 0% -> 0%
where the time goes in v1:
time: 109 us
  Pallas kernels  105 us (96%)
  local copies, waits for them, and re-layouts  3.36 us (3%)
    pallas_call x1, Pallas kernels, on_device(): pl.pallas_call(kernel, out_shape=(jax.ShapeDtypeStruct((hidden, features)...  105 us
    unnamed x4, local copies, waits for them, and re-layouts  3.36 us

profile of v1, /device:TPU:1, one launch (start us, length us, event | category | flops | bytes accessed | tf_op | source)
XLA Modules:
  0.0 108.9 jit_solution(5221146529028036074)
XLA Ops:
  0.6 104.9 %diloco.1 = (bf16[448,832]{1,0:T(8,128)(2,1)}, f32[448,832]{1,0:T(8,128)}) custom-call(bf16[832,256]{1,0:T(8,128)(2,1)} %bitcast.17, bf16[448,8192]{1,0:T(8,128)(2,1)} %bitcast.9, f32[448,832]{1,0:T(8,128)} %bitcast.11, f32[448,832]{1,0:T(8,128)} %bitcast.12, f32[448,832]{1,0:T(8,128)} %bitcast.13, f32[448,832]{1,0:T(8,128)} %bitcast.14, f32[448,832]{1,0:T(8,128)} %bitcast.15), custom_call_target="tpu_custom_call" | custom-call | tf_op jit(solution)/shard_map/diloco/pallas_call | solution.py:360
  105.5 0.0 copy-start
  105.5 2.2 %copy.11 = bf16[832,448]{0,1:T(8,128)(2,1)} copy(bf16[832,448]{0,1:T(8,128)(2,1)} %bitcast.16) | data formatting | bytes 1490944
  107.7 0.0 copy-done
  107.7 1.2 %copy.12 = f32[832,448]{0,1:T(8,128)} copy(f32[832,448]{0,1:T(8,128)S(1)} %bitcast.10) | data formatting | bytes 2981888
Async XLA Ops:
  105.5 2.2 %copy-start = (f32[448,832]{1,0:T(8,128)S(1)}, f32[448,832]{1,0:T(8,128)}, u32[]{:S(2)}) copy-start(f32[448,832]{1,0:T(8,128)} %get-tuple-element.5) | copy-start | bytes 4472836

commit v2 on v1

v2 whole, which is shorter than its diff:
```python
import heapq

import jax
import jax.numpy as jnp
from jax import lax
from jax.experimental import pallas as pl
from jax.experimental.pallas import tpu as pltpu
from jax.sharding import PartitionSpec as P

BETA_ONE = 0.9
BETA_TWO = 0.95
BIAS_ONE = 0.9999734386
BIAS_TWO = 0.9940794708
EPSILON = 1e-08
INNER_RATE = 0.25
DECAY_RATE = 0.1
OUTER_RATE = 0.7
NESTEROV = 0.9

MESH = pl.DeviceIdType.MESH
NX, NZ, NC = 4, 4, 2
RING = (0, -1, 1, 2)

PHASES = ((256, "z"), (128, "x"), (256, "z"), (128, "z"), (64, "z"))
DIRECT = (4,)
RATE = {"x": 44e3, "z": 22e3, "d": 300e3, "y": 75e3}
DELAY = {"x": 2.0, "z": 2.7, "d": 1.0, "y": 2.5}
LEAD, BACKLOG = 1, 1.0
TILE_US, UPDATE_US, SEND_US = 3.5, 4.0, 0.02
OTHER = {"x": "z", "z": "x"}


def offset(first, a, b):
    return (a, b) if first == "x" else (b, a)


def transfers(p, first):
    second = OTHER[first]
    moves = {
        (1, p, 1): (first, (0, 0), "all", 1, offset(first, -1, 0)),
        (1, p, -1): (first, (0, 0), "all", -1, offset(first, 1, 0)),
        (2, p, 1): (first, offset(first, -1, 0), "low", 1, offset(first, 2, 0)),
        (2, p, -1): (first, offset(first, 1, 0), "high", -1, offset(first, 2, 0)),
    }
    for a in RING:
        moves[3, p, 1, a] = (second, offset(first, a, 0), "all", 1, offset(first, a, -1))
        moves[3, p, -1, a] = (second, offset(first, a, 0), "all", -1, offset(first, a, 1))
        moves[4, p, 1, a] = (second, offset(first, a, -1), "low", 1, offset(first, a, 2))
        moves[4, p, -1, a] = (second, offset(first, a, 1), "high", -1, offset(first, a, 2))
        for b in RING:
            moves[(5, p, *offset(first, a, b))] = ("d", offset(first, a, b), "all", 0, offset(first, a, b))
    return moves


GROUPS = ((0, -1), (1, 2))


def plan(phases, hidden):
    total = sum(f for f, _ in phases)
    moves, rules, tasks = {}, [], []
    for p, (_, first) in enumerate(phases):
        moves.update(transfers(p, first))
        third = lambda a: [(3, p, 1, a), (3, p, -1, a)]
        follow = lambda a, b: (5, p, *offset(first, a, b))
        rules.append(([(1, p, 1)], [(2, p, 1)] + third(-1) + [follow(-1, 0)]))
        rules.append(([(1, p, -1)], [(2, p, -1)] + third(1) + [follow(1, 0)]))
        rules.append(([(2, p, 1), (2, p, -1)], third(2) + [follow(2, 0)]))
        for a in RING:
            rules.append(([(3, p, 1, a)], [(4, p, 1, a), follow(a, -1)]))
            rules.append(([(3, p, -1, a)], [(4, p, -1, a), follow(a, 1)]))
            rules.append(([(4, p, 1, a), (4, p, -1, a)], [follow(a, 2)]))
        size = phases[p][0]
        needs_all = set()
        for dx in RING:
            for group in GROUPS:
                needs = {n for n, m in moves.items() if n[1] == p and m[4][0] == dx and m[4][1] in group}
                tasks.append((("mm", p, dx, group), needs, TILE_US / 8 * -(-size // 256)))
                needs_all.add(("mm", p, dx, group))
        share = UPDATE_US * size / total
        tasks.append((("update", p), needs_all, share))
        if p in DIRECT:
            tasks.append((("reduce", p), {("RS", p)}, share / 8))
        else:
            tasks.append((("halve", p), {("RS", p)}, share / 8))
            tasks.append((("reduce", p), {("PAIR", p)}, share / 16))
            tasks.append((("forward", p), {("AGZ", p)}, 0.02))
        tasks.append((("final", p), {("AG", p)}, share / 2))

    steps, arrivals, free, done, arrived, waited = [], [], {}, set(), set(), set()
    pending = {}
    clock, serial = 0.0, 0

    def urgency(name):
        stage, p = name[:2]
        return p - LEAD * (stage < 3) - 0.25 * (stage in (2, 4)), stage != 3 or name[3] != 2

    def request(names):
        for name in names:
            link, _, _, way, _ = moves[name]
            pending.setdefault((link, way), []).append(name)

    def push(name, lane, took, delay):
        nonlocal serial
        free[lane] = max(clock, free.get(lane, 0.0)) + took
        heapq.heappush(arrivals, (free[lane] + delay, serial, name))
        serial += 1

    def pump():
        nonlocal clock
        sent = []
        for lane, names in pending.items():
            while names and free.get(lane, 0.0) - clock < BACKLOG:
                name = min(names, key=urgency)
                names.remove(name)
                size = phases[name[1]][0] * 512 * (1.0 if moves[name][2] == "all" else 0.5)
                push(name, lane, size / RATE[lane[0]], DELAY[lane[0]])
                clock += SEND_US
                sent.append(name)
        if sent:
            steps.append(("send", tuple(sent)))

    def exchange(kind, p):
        size = phases[p][0] * hidden * 4
        if kind == "RS" or kind == "AG" and p in DIRECT:
            push((kind, p), "y", size * 0.75 / RATE["y"], DELAY["y"] + (p in DIRECT))
        elif kind == "forward":
            push(("AG", p), "y", size * 0.375 / RATE["y"], DELAY["y"])
        elif kind == "PAIR":
            push((kind, p), ("z", 1), size / 8 / RATE["x"], DELAY["x"])
        else:
            push(("AGY", p), "y", size * 0.375 / RATE["y"], DELAY["y"])
            push(("AGZ", p), ("z", 1), size / 8 / RATE["x"], DELAY["x"])

    for p, (_, first) in enumerate(phases):
        request([(1, p, 1), (1, p, -1), (3, p, 1, 0), (3, p, -1, 0), (5, p, 0, 0)])
    pump()
    rank = {"reduce": 0, "halve": 1, "forward": 2, "update": 3, "mm": 4, "final": 5}
    after = {"update": "RS", "halve": "PAIR", "reduce": "AG", "forward": "forward"}
    while rules or tasks:
        while arrivals and arrivals[0][0] <= clock:
            arrived.add(heapq.heappop(arrivals)[2])
        rule = next((r for r in rules if set(r[0]) <= arrived), None)
        if rule:
            rules.remove(rule)
            for name in rule[0]:
                waited.add(name)
                steps.append(("wait", name))
            request(rule[1])
            pump()
            continue
        ready = [t for t in tasks if t[1] <= (arrived | done)]
        if ready:
            task = min(ready, key=lambda t: (rank[t[0][0]], t[0][1]))
            tasks.remove(task)
            for name in sorted(task[1] - waited - done, key=str):
                waited.add(name)
                steps.append(("wait", name))
            steps.append(task[0])
            clock += task[2]
            done.add(task[0])
            if task[0][0] in after:
                exchange(after[task[0][0]], task[0][1])
            pump()
            continue
        clock = arrivals[0][0]
        pump()
    return steps, moves, clock


def make_kernel(phases, features, hidden, tokens, replicas):
    steps, moves, _ = plan(phases, hidden)
    sizes = [f for f, _ in phases]
    starts = [sum(sizes[:p]) for p in range(len(sizes))]
    index = {name: i for i, name in enumerate(sorted(moves, key=str))}
    share = hidden // replicas
    ny = replicas // 2

    def kernel(
        act, grad, w_hbm, m_hbm, v_hbm, an_hbm, mo_hbm, reb_ref, mom_ref,
        held, g_buf, w_buf, m_buf, v_buf, an_buf, mo_buf, acc, landed, mean,
        out_sem, in_sem, rs_out, rs_in, ag_out, ag_in, load_sem,
    ):
        me_r, me_t = lax.axis_index("replica"), lax.axis_index("tensor")
        core = lax.rem(me_t, NC)
        zh = lax.rem(me_t // NC, NZ)
        x = me_t // (NC * NZ)
        zl = me_r // ny
        y = lax.rem(me_r, ny)

        def slot(dx, dz, c):
            return (lax.rem(x + dx + NX, NX) * NZ + lax.rem(zh + dz + NZ, NZ)) * NC + c

        def device(dx, dz, c):
            return {"replica": me_r, "tensor": slot(dx, dz, c)}

        def place(j, sign=1):
            there = lax.rem(zl + j // ny, 2)
            return there, lax.rem(y + sign * (j % ny) + ny, ny)

        def replica(j):
            there, row = place(j)
            return {"replica": there * ny + row, "tensor": me_t}

        loads = [
            pltpu.make_async_copy(src, dst, load_sem.at[i])
            for i, (src, dst) in enumerate(
                ((act, held.at[me_t]), (grad, g_buf), (w_hbm, w_buf), (m_hbm, m_buf), (v_hbm, v_buf), (an_hbm, an_buf), (mo_hbm, mo_buf))
            )
        ]
        for load in loads:
            load.start()

        barrier = pltpu.get_barrier_semaphore()
        friends = [device(0, 1, core), device(0, -1, core), device(1, 0, core), device(-1, 0, core), device(0, 0, 1 - core)]
        friends += [replica(j) for j in range(1, replicas)]
        for friend in friends:
            pl.semaphore_signal(barrier, inc=1, device_id=friend, device_id_type=MESH)
        pl.semaphore_wait(barrier, len(friends))

        def rows_of(name):
            p, part = name[1], moves[name][2]
            half = sizes[p] // 2
            begin = starts[p] + (half if part == "high" else 0)
            return pl.ds(begin, sizes[p] if part == "all" else half)

        def outgoing(name):
            link, source, _, way, _ = moves[name]
            rows = rows_of(name)
            there = slot(*source, core)
            target = {"x": device(way, 0, core), "z": device(0, way, core), "d": device(0, 0, 1 - core)}[link]
            src = act.at[rows] if source == (0, 0) else held.at[there, rows]
            return pltpu.make_async_remote_copy(
                src_ref=src,
                dst_ref=held.at[there, rows],
                send_sem=out_sem.at[index[name]],
                recv_sem=in_sem.at[index[name]],
                device_id=target,
                device_id_type=MESH,
            )

        def incoming(name):
            link, _, _, _, got = moves[name]
            spot = held.at[slot(*got, 1 - core if link == "d" else core), rows_of(name)]
            return pltpu.make_async_remote_copy(
                src_ref=spot,
                dst_ref=spot,
                send_sem=out_sem.at[index[name]],
                recv_sem=in_sem.at[index[name]],
                device_id=device(0, 0, 1 - core),
                device_id_type=MESH,
            )

        def columns(p):
            return pl.ds(starts[p], sizes[p])

        def shares(place, count=1):
            there, row = place
            return pl.ds(pl.multiple_of(row * 2 * share + (there * share if count == 1 else 0), 8), count * share)

        def remote(src, dst, out, into, target):
            return pltpu.make_async_remote_copy(
                src_ref=src, dst_ref=dst, send_sem=out, recv_sem=into, device_id=target, device_id_type=MESH
            )

        def scatter(p):
            cols = columns(p)
            if p in DIRECT:
                for j in range(1, replicas):
                    at = j - 1
                    dst = landed.at[pl.ds(at * share, share), cols]
                    yield remote(acc.at[shares(place(j)), cols], dst, rs_out.at[p, at], rs_in.at[p, at], replica(j))
            else:
                for j in range(1, ny):
                    at = j - 1
                    dst = landed.at[pl.ds(at * 2 * share, 2 * share), cols]
                    yield remote(acc.at[shares(place(j), 2), cols], dst, rs_out.at[p, at], rs_in.at[p, at], replica(j))

        def pair(p):
            cols, at = columns(p), ny - 1
            dst = landed.at[pl.ds(at * 2 * share, share), cols]
            return remote(acc.at[shares(place(ny)), cols], dst, rs_out.at[p, at], rs_in.at[p, at], replica(ny))

        def spread(p, sent=True, offsets=None):
            cols = columns(p)
            for j in offsets or range(1, replicas if p in DIRECT else ny + 1):
                ref = mean.at[shares((zl, y) if sent else place(j, -1)), cols]
                yield remote(ref, ref, ag_out.at[p, j - 1], ag_in.at[p, j - 1], replica(j))

        def forward(p, sent=True):
            cols = columns(p)
            for j in range(1, ny):
                there, row = place(j, -1)
                ref = mean.at[shares((1 - zl, y) if sent else (1 - zl, row)), cols]
                yield remote(ref, ref, ag_out.at[p, ny + j - 1], ag_in.at[p, ny + j - 1], replica(j))

        def matmul(p, dx, group, first):
            cols = columns(p)

            def product(dz, c):
                block = slot(dx, dz, c)
                left = g_buf[:, pl.ds(pl.multiple_of(block * tokens, tokens), tokens)]
                return lax.dot_general(left, held[block, cols, :], (((1,), (1,)), ((), ())), preferred_element_type=jnp.float32)

            low = min(group)
            if first:
                acc[:, cols] = product(low, 0) + product(low, 1)

            @pl.loop(1 if first else 0, len(group))
            def _(i):
                acc[:, cols] += product(low + i, 0) + product(low + i, 1)

        def update(p):
            cols = columns(p)
            step = 32

            @pl.loop(0, hidden // step)
            def _(i):
                rows = pl.ds(pl.multiple_of(i * step, step), step)
                gradient = acc[rows, cols]
                weights = w_buf[rows, cols]
                moment_one = BETA_ONE * m_buf[rows, cols] + (1.0 - BETA_ONE) * gradient
                moment_two = BETA_TWO * v_buf[rows, cols] + (1.0 - BETA_TWO) * gradient * gradient
                size = moment_one * (1.0 / BIAS_ONE) / (jnp.sqrt(moment_two * (1.0 / BIAS_TWO)) + EPSILON)
                updated = weights - INNER_RATE * (size + DECAY_RATE * weights)
                acc[rows, cols] = an_buf[rows, cols] - updated

        def halve(p):
            cols = columns(p)
            for there in (1 - zl, zl):
                rows = shares((there, y))
                total = acc[rows, cols]
                for j in range(ny - 1):
                    total = total + landed[pl.ds(pl.multiple_of(j * 2 * share + there * share, 8), share), cols]
                acc[rows, cols] = total

        def reduce(p):
            cols = columns(p)
            rows = shares((zl, y))
            total = acc[rows, cols]
            for at in range(replicas - 1) if p in DIRECT else (replicas - 2,):
                total = total + landed[pl.ds(at * share, share), cols]
            mean[rows, cols] = total * (1.0 / replicas)

        def final(p):
            cols = columns(p)
            step = 32

            @pl.loop(0, hidden // step)
            def _(i):
                rows = pl.ds(pl.multiple_of(i * step, step), step)
                pseudo_mean = mean[rows, cols]
                new_momentum = NESTEROV * mo_buf[rows, cols] + pseudo_mean
                mom_ref[rows, cols] = new_momentum
                rebuilt = an_buf[rows, cols] - OUTER_RATE * (pseudo_mean + NESTEROV * new_momentum)
                reb_ref[rows, cols] = rebuilt.astype(reb_ref.dtype)

        multiplied, loaded = set(), set()

        def load_wait(*which):
            for i in which:
                if i not in loaded:
                    loaded.add(i)
                    loads[i].wait()

        def wait(name):
            kind, p = name[:2]
            if kind == "RS":
                for copy in scatter(p):
                    copy.wait_recv()
            elif kind == "PAIR":
                pair(p).wait_recv()
            elif kind == "AGZ":
                for copy in spread(p, False, (ny,)):
                    copy.wait_recv()
            elif kind == "AG":
                for copy in spread(p, False, range(1, replicas if p in DIRECT else ny)):
                    copy.wait_recv()
                if p not in DIRECT:
                    for copy in forward(p, False):
                        copy.wait_recv()
            else:
                incoming(name).wait_recv()

        for kind, *rest in steps:
            p = rest[0]
            if kind == "send":
                for name in rest[0]:
                    outgoing(name).start()
            elif kind == "forward":
                for copy in forward(p):
                    copy.start()
            elif kind == "wait":
                wait(rest[0])
            elif kind == "mm":
                load_wait(0, 1)
                matmul(*rest, p not in multiplied)
                multiplied.add(p)
            elif kind == "update":
                load_wait(2, 3, 4, 5)
                update(p)
                for copy in scatter(p):
                    copy.start()
            elif kind == "halve":
                halve(p)
                pair(p).start()
            elif kind == "reduce":
                reduce(p)
                for copy in spread(p):
                    copy.start()
            elif kind == "final":
                load_wait(6)
                final(p)
        for name in index:
            outgoing(name).wait_send()
        for p in range(len(sizes)):
            copies = [*scatter(p), *spread(p)]
            if p not in DIRECT:
                copies += [pair(p), *forward(p)]
            for copy in copies:
                copy.wait_send()

    count = len(index)
    full = (hidden, features)
    scratch = [
        pltpu.VMEM((NX * NZ * NC, features, tokens), jnp.bfloat16),
        pltpu.VMEM((hidden, NX * NZ * NC * tokens), jnp.bfloat16),
        *[pltpu.VMEM(full, jnp.float32)] * 5,
        pltpu.VMEM(full, jnp.float32),
        pltpu.VMEM(((replicas - 1) * share, features), jnp.float32),
        pltpu.VMEM(full, jnp.float32),
        pltpu.SemaphoreType.DMA((count,)),
        pltpu.SemaphoreType.DMA((count,)),
        *[pltpu.SemaphoreType.DMA((len(sizes), replicas - 1))] * 4,
        pltpu.SemaphoreType.DMA((7,)),
    ]
    return kernel, scratch


def on_device(activations, out_grad, master_weights, first_moment, second_moment, anchor, outer_momentum):
    tokens, features = activations.shape
    hidden = out_grad.shape[1]
    replicas = lax.axis_size("replica")
    kernel, scratch = make_kernel(PHASES, features, hidden, tokens, replicas)
    rebuilt, momentum = pl.pallas_call(
        kernel,
        out_shape=(
            jax.ShapeDtypeStruct((hidden, features), jnp.bfloat16),
            jax.ShapeDtypeStruct((hidden, features), jnp.float32),
        ),
        in_specs=[pl.BlockSpec(memory_space=pl.ANY)] * 7,
        out_specs=(pl.BlockSpec(memory_space=pltpu.VMEM),) * 2,
        scratch_shapes=scratch,
        compiler_params=pltpu.CompilerParams(collective_id=0, has_side_effects=True, vmem_limit_bytes=60 * 2**20),
        name="diloco",
    )(*(a.T for a in (activations, out_grad, master_weights, first_moment, second_moment, anchor, outer_momentum)))
    return rebuilt.T, momentum.T


def solution(mesh):
    placed = (
        P(("replica", "tensor"), None),
        P("replica", "tensor"),
        P("replica", "tensor"),
        P("replica", "tensor"),
        P("replica", "tensor"),
        P(None, "tensor"),
        P(None, "tensor"),
    )
    return jax.shard_map(
        on_device,
        mesh=mesh,
        in_specs=placed,
        out_specs=(P(None, "tensor"), P(None, "tensor")),
        check_vma=False,
    )
```

time: 109 us -> 97.6 us (0.90)
  Pallas kernels: 105 us -> 93.5 us
    pallas_call x1, Pallas kernels: 105 us -> 93.5 us  [on_device(): pl.pallas_call(kernel, out_shape=(jax.ShapeDtypeStruct((hidden, features)...]
where the time goes in v2:
time: 97.6 us; the launch traced here: 97.5 us
  Pallas kernels  93.5 us (96%)
  local copies, waits for them, and re-layouts  3.36 us (3%)
    pallas_call x1, Pallas kernels, on_device(): pl.pallas_call(kernel, out_shape=(jax.ShapeDtypeStruct((hidden, features)...  93.5 us
    unnamed x4, local copies, waits for them, and re-layouts  3.36 us

profile of v2, /device:TPU:1, one launch (start us, length us, event | category | flops | bytes accessed | tf_op | source)
XLA Modules:
  0.0 97.5 jit_solution(2498168482947429509)
XLA Ops:
  0.6 93.5 %diloco.1 = (bf16[448,832]{1,0:T(8,128)(2,1)}, f32[448,832]{1,0:T(8,128)}) custom-call(bf16[832,256]{1,0:T(8,128)(2,1)} %bitcast.17, bf16[448,8192]{1,0:T(8,128)(2,1)} %bitcast.9, f32[448,832]{1,0:T(8,128)} %bitcast.11, f32[448,832]{1,0:T(8,128)} %bitcast.12, f32[448,832]{1,0:T(8,128)} %bitcast.13, f32[448,832]{1,0:T(8,128)} %bitcast.14, f32[448,832]{1,0:T(8,128)} %bitcast.15), custom_call_target="tpu_custom_call" | custom-call | tf_op jit(solution)/shard_map/diloco/pallas_call | solution.py:444
  94.1 0.0 copy-start
  94.1 2.2 %copy.11 = bf16[832,448]{0,1:T(8,128)(2,1)} copy(bf16[832,448]{0,1:T(8,128)(2,1)} %bitcast.16) | data formatting | bytes 1490944
  96.3 0.0 copy-done
  96.3 1.2 %copy.12 = f32[832,448]{0,1:T(8,128)} copy(f32[832,448]{0,1:T(8,128)S(1)} %bitcast.10) | data formatting | bytes 2981888
Async XLA Ops:
  94.1 2.2 %copy-start = (f32[448,832]{1,0:T(8,128)S(1)}, f32[448,832]{1,0:T(8,128)}, u32[]{:S(2)}) copy-start(f32[448,832]{1,0:T(8,128)} %get-tuple-element.5) | copy-start | bytes 4472836

commit v3 on v2

--- a/solution.py
+++ b/solution.py
@@ -22,7 +22,7 @@
 RING = (0, -1, 1, 2)
 
 PHASES = ((256, "z"), (128, "x"), (256, "z"), (128, "z"), (64, "z"))
-DIRECT = (4,)
+MODES = ("yz", "yz", "yz", "yz", "all")
 RATE = {"x": 44e3, "z": 22e3, "d": 300e3, "y": 75e3}
 DELAY = {"x": 2.0, "z": 2.7, "d": 1.0, "y": 2.5}
 LEAD, BACKLOG = 1, 1.0
@@ -78,13 +78,13 @@
                 needs_all.add(("mm", p, dx, group))
         share = UPDATE_US * size / total
         tasks.append((("update", p), needs_all, share))
-        if p in DIRECT:
+        if MODES[p] == "all":
             tasks.append((("reduce", p), {("RS", p)}, share / 8))
         else:
             tasks.append((("halve", p), {("RS", p)}, share / 8))
             tasks.append((("reduce", p), {("PAIR", p)}, share / 16))
             tasks.append((("forward", p), {("AGZ", p)}, 0.02))
-        tasks.append((("final", p), {("AG", p)}, share / 2))
+        tasks.append((("final", p), {("AG", p)}, 0.02))
 
     steps, arrivals, free, done, arrived, waited = [], [], {}, set(), set(), set()
     pending = {}
@@ -121,15 +121,21 @@
 
     def exchange(kind, p):
         size = phases[p][0] * hidden * 4
-        if kind == "RS" or kind == "AG" and p in DIRECT:
-            push((kind, p), "y", size * 0.75 / RATE["y"], DELAY["y"] + (p in DIRECT))
-        elif kind == "forward":
-            push(("AG", p), "y", size * 0.375 / RATE["y"], DELAY["y"])
+        y_part = lambda name, part: push((name, p), "y", size * part / RATE["y"], DELAY["y"] + (MODES[p] == "all"))
+        z_part = lambda name, part: push((name, p), ("z", 1), size * part / RATE["x"], DELAY["x"])
+        if MODES[p] == "all":
+            y_part(kind, 0.75)
+        elif MODES[p] == "zy":
+            {"RS": z_part, "PAIR": y_part, "AG": y_part, "forward": z_part}[kind](
+                {"AG": "AGZ", "forward": "AG"}.get(kind, kind), 0.5 if kind in ("RS", "forward") else 0.375
+            )
+        elif kind == "AG":
+            y_part("AGY", 0.375)
+            z_part("AGZ", 0.125)
         elif kind == "PAIR":
-            push((kind, p), ("z", 1), size / 8 / RATE["x"], DELAY["x"])
+            z_part(kind, 0.125)
         else:
-            push(("AGY", p), "y", size * 0.375 / RATE["y"], DELAY["y"])
-            push(("AGZ", p), ("z", 1), size / 8 / RATE["x"], DELAY["x"])
+            y_part("AG" if kind == "forward" else kind, 0.375 if kind == "forward" else 0.75)
 
     for p, (_, first) in enumerate(phases):
         request([(1, p, 1), (1, p, -1), (3, p, 1, 0), (3, p, -1, 0), (5, p, 0, 0)])
@@ -176,9 +182,9 @@
     ny = replicas // 2
 
     def kernel(
-        act, grad, w_hbm, m_hbm, v_hbm, an_hbm, mo_hbm, reb_ref, mom_ref,
-        held, g_buf, w_buf, m_buf, v_buf, an_buf, mo_buf, acc, landed, mean,
-        out_sem, in_sem, rs_out, rs_in, ag_out, ag_in, load_sem,
+        act, grad, w_hbm, m_hbm, v_hbm, an_hbm, mean_hbm,
+        held, g_buf, w_buf, m_buf, v_buf, an_buf, acc, landed, mean,
+        out_sem, in_sem, rs_out, rs_in, ag_out, ag_in, load_sem, put_sem,
     ):
         me_r, me_t = lax.axis_index("replica"), lax.axis_index("tensor")
         core = lax.rem(me_t, NC)
@@ -204,7 +210,7 @@
         loads = [
             pltpu.make_async_copy(src, dst, load_sem.at[i])
             for i, (src, dst) in enumerate(
-                ((act, held.at[me_t]), (grad, g_buf), (w_hbm, w_buf), (m_hbm, m_buf), (v_hbm, v_buf), (an_hbm, an_buf), (mo_hbm, mo_buf))
+                ((act, held.at[me_t]), (grad, g_buf), (w_hbm, w_buf), (m_hbm, m_buf), (v_hbm, v_buf), (an_hbm, an_buf))
             )
         ]
         for load in loads:
@@ -253,45 +259,61 @@
         def columns(p):
             return pl.ds(starts[p], sizes[p])
 
-        def shares(place, count=1):
+        def shares(p, place):
             there, row = place
-            return pl.ds(pl.multiple_of(row * 2 * share + (there * share if count == 1 else 0), 8), count * share)
+            return pl.ds(pl.multiple_of((there * ny + row if MODES[p] == "zy" else row * 2 + there) * share, 8), share)
+
+        def both(row):
+            return pl.ds(pl.multiple_of(row * 2 * share, 8), 2 * share)
+
+        def half(there):
+            return pl.ds(pl.multiple_of(there * ny * share, 8), ny * share)
 
         def remote(src, dst, out, into, target):
             return pltpu.make_async_remote_copy(
                 src_ref=src, dst_ref=dst, send_sem=out, recv_sem=into, device_id=target, device_id_type=MESH
             )
 
+        def landing(at, count=1):
+            return pl.ds(at * share, count * share)
+
+        def summand(p, rows, spot, at, j):
+            cols = columns(p)
+            return remote(acc.at[rows, cols], landed.at[spot, cols], rs_out.at[p, at], rs_in.at[p, at], replica(j))
+
         def scatter(p):
-            cols = columns(p)
-            if p in DIRECT:
-                for j in range(1, replicas):
-                    at = j - 1
-                    dst = landed.at[pl.ds(at * share, share), cols]
-                    yield remote(acc.at[shares(place(j)), cols], dst, rs_out.at[p, at], rs_in.at[p, at], replica(j))
-            else:
-                for j in range(1, ny):
-                    at = j - 1
-                    dst = landed.at[pl.ds(at * 2 * share, 2 * share), cols]
-                    yield remote(acc.at[shares(place(j), 2), cols], dst, rs_out.at[p, at], rs_in.at[p, at], replica(j))
+            if MODES[p] == "all":
+                return [summand(p, shares(p, place(j)), landing(j - 1), j - 1, j) for j in range(1, replicas)]
+            if MODES[p] == "zy":
+                return [summand(p, half(1 - zl), landing(0, ny), 0, ny)]
+            return [summand(p, both(place(j)[1]), landing(2 * (j - 1), 2), j - 1, j) for j in range(1, ny)]
 
         def pair(p):
-            cols, at = columns(p), ny - 1
-            dst = landed.at[pl.ds(at * 2 * share, share), cols]
-            return remote(acc.at[shares(place(ny)), cols], dst, rs_out.at[p, at], rs_in.at[p, at], replica(ny))
+            if MODES[p] == "all":
+                return []
+            if MODES[p] == "zy":
+                return [summand(p, shares(p, place(j)), landing(ny + j - 1), j, j) for j in range(1, ny)]
+            return [summand(p, shares(p, place(ny)), landing(replicas - 2), ny - 1, ny)]
+
+        def result(p, rows, at, j):
+            ref = mean.at[rows, columns(p)]
+            return remote(ref, ref, ag_out.at[p, at], ag_in.at[p, at], replica(j))
 
         def spread(p, sent=True, offsets=None):
-            cols = columns(p)
-            for j in offsets or range(1, replicas if p in DIRECT else ny + 1):
-                ref = mean.at[shares((zl, y) if sent else place(j, -1)), cols]
-                yield remote(ref, ref, ag_out.at[p, j - 1], ag_in.at[p, j - 1], replica(j))
+            last = {"all": replicas, "zy": ny, "yz": ny + 1}[MODES[p]]
+            return [
+                result(p, shares(p, (zl, y) if sent else place(j, -1)), j - 1, j) for j in offsets or range(1, last)
+            ]
 
         def forward(p, sent=True):
-            cols = columns(p)
-            for j in range(1, ny):
-                there, row = place(j, -1)
-                ref = mean.at[shares((1 - zl, y) if sent else (1 - zl, row)), cols]
-                yield remote(ref, ref, ag_out.at[p, ny + j - 1], ag_in.at[p, ny + j - 1], replica(j))
+            if MODES[p] == "all":
+                return []
+            if MODES[p] == "zy":
+                return [result(p, half(zl if sent else 1 - zl), ny - 1, ny)]
+            return [
+                result(p, shares(p, (1 - zl, y) if sent else (1 - zl, place(j, -1)[1])), ny + j - 1, j)
+                for j in range(1, ny)
+            ]
 
         def matmul(p, dx, group, first):
             cols = columns(p)
@@ -326,33 +348,25 @@
 
         def halve(p):
             cols = columns(p)
-            for there in (1 - zl, zl):
-                rows = shares((there, y))
-                total = acc[rows, cols]
-                for j in range(ny - 1):
-                    total = total + landed[pl.ds(pl.multiple_of(j * 2 * share + there * share, 8), share), cols]
-                acc[rows, cols] = total
+            if MODES[p] == "zy":
+                for row in range(ny):
+                    rows = shares(p, (zl, row))
+                    acc[rows, cols] = acc[rows, cols] + landed[landing(row), cols]
+            else:
+                for there in (1 - zl, zl):
+                    rows = shares(p, (there, y))
+                    total = acc[rows, cols]
+                    for j in range(ny - 1):
+                        total = total + landed[pl.ds(pl.multiple_of((j * 2 + there) * share, 8), share), cols]
+                    acc[rows, cols] = total
 
         def reduce(p):
             cols = columns(p)
-            rows = shares((zl, y))
+            rows = shares(p, (zl, y))
             total = acc[rows, cols]
-            for at in range(replicas - 1) if p in DIRECT else (replicas - 2,):
-                total = total + landed[pl.ds(at * share, share), cols]
+            for at in {"all": range(replicas - 1), "zy": range(ny, replicas - 1), "yz": (replicas - 2,)}[MODES[p]]:
+                total = total + landed[landing(at), cols]
             mean[rows, cols] = total * (1.0 / replicas)
-
-        def final(p):
-            cols = columns(p)
-            step = 32
-
-            @pl.loop(0, hidden // step)
-            def _(i):
-                rows = pl.ds(pl.multiple_of(i * step, step), step)
-                pseudo_mean = mean[rows, cols]
-                new_momentum = NESTEROV * mo_buf[rows, cols] + pseudo_mean
-                mom_ref[rows, cols] = new_momentum
-                rebuilt = an_buf[rows, cols] - OUTER_RATE * (pseudo_mean + NESTEROV * new_momentum)
-                reb_ref[rows, cols] = rebuilt.astype(reb_ref.dtype)
 
         multiplied, loaded = set(), set()
 
@@ -364,31 +378,29 @@
 
         def wait(name):
             kind, p = name[:2]
-            if kind == "RS":
-                for copy in scatter(p):
-                    copy.wait_recv()
-            elif kind == "PAIR":
-                pair(p).wait_recv()
-            elif kind == "AGZ":
-                for copy in spread(p, False, (ny,)):
-                    copy.wait_recv()
-            elif kind == "AG":
-                for copy in spread(p, False, range(1, replicas if p in DIRECT else ny)):
-                    copy.wait_recv()
-                if p not in DIRECT:
-                    for copy in forward(p, False):
-                        copy.wait_recv()
-            else:
-                incoming(name).wait_recv()
+            copies = {
+                "RS": lambda: scatter(p),
+                "PAIR": lambda: pair(p),
+                "AGZ": lambda: spread(p, False, (ny,) if MODES[p] == "yz" else None),
+                "AG": lambda: {
+                    "all": lambda: spread(p, False),
+                    "zy": lambda: forward(p, False),
+                    "yz": lambda: spread(p, False, range(1, ny)) + forward(p, False),
+                }[MODES[p]](),
+            }.get(kind, lambda: [incoming(name)])
+            for copy in copies():
+                copy.wait_recv()
+
+        def start(copies):
+            for copy in copies:
+                copy.start()
 
         for kind, *rest in steps:
             p = rest[0]
             if kind == "send":
-                for name in rest[0]:
-                    outgoing(name).start()
+                start(outgoing(name) for name in rest[0])
             elif kind == "forward":
-                for copy in forward(p):
-                    copy.start()
+                start(forward(p))
             elif kind == "wait":
                 wait(rest[0])
             elif kind == "mm":
@@ -398,25 +410,21 @@
             elif kind == "update":
                 load_wait(2, 3, 4, 5)
                 update(p)
-                for copy in scatter(p):
-                    copy.start()
+                start(scatter(p))
             elif kind == "halve":
                 halve(p)
-                pair(p).start()
+                start(pair(p))
             elif kind == "reduce":
                 reduce(p)
-                for copy in spread(p):
-                    copy.start()
+                start(spread(p))
             elif kind == "final":
-                load_wait(6)
-                final(p)
+                pltpu.make_async_copy(mean.at[:, columns(p)], mean_hbm.at[:, columns(p)], put_sem.at[p]).start()
+        for p in range(len(sizes)):
+            pltpu.make_async_copy(mean.at[:, columns(p)], mean_hbm.at[:, columns(p)], put_sem.at[p]).wait()
         for name in index:
             outgoing(name).wait_send()
         for p in range(len(sizes)):
-            copies = [*scatter(p), *spread(p)]
-            if p not in DIRECT:
-                copies += [pair(p), *forward(p)]
-            for copy in copies:
+            for copy in [*scatter(p), *pair(p), *spread(p), *forward(p)]:
                 copy.wait_send()
 
     count = len(index)
@@ -424,14 +432,15 @@
     scratch = [
         pltpu.VMEM((NX * NZ * NC, features, tokens), jnp.bfloat16),
         pltpu.VMEM((hidden, NX * NZ * NC * tokens), jnp.bfloat16),
-        *[pltpu.VMEM(full, jnp.float32)] * 5,
+        *[pltpu.VMEM(full, jnp.float32)] * 4,
         pltpu.VMEM(full, jnp.float32),
         pltpu.VMEM(((replicas - 1) * share, features), jnp.float32),
         pltpu.VMEM(full, jnp.float32),
         pltpu.SemaphoreType.DMA((count,)),
         pltpu.SemaphoreType.DMA((count,)),
         *[pltpu.SemaphoreType.DMA((len(sizes), replicas - 1))] * 4,
-        pltpu.SemaphoreType.DMA((7,)),
+        pltpu.SemaphoreType.DMA((6,)),
+        pltpu.SemaphoreType.DMA((len(sizes),)),
     ]
     return kernel, scratch
 
@@ -441,19 +450,19 @@
     hidden = out_grad.shape[1]
     replicas = lax.axis_size("replica")
     kernel, scratch = make_kernel(PHASES, features, hidden, tokens, replicas)
-    rebuilt, momentum = pl.pallas_call(
+    operands = (activations, out_grad, master_weights, first_moment, second_moment, anchor)
+    pseudo_mean = pl.pallas_call(
         kernel,
-        out_shape=(
-            jax.ShapeDtypeStruct((hidden, features), jnp.bfloat16),
-            jax.ShapeDtypeStruct((hidden, features), jnp.float32),
-        ),
-        in_specs=[pl.BlockSpec(memory_space=pl.ANY)] * 7,
-        out_specs=(pl.BlockSpec(memory_space=pltpu.VMEM),) * 2,
+        out_shape=jax.ShapeDtypeStruct((hidden, features), jnp.float32),
+        in_specs=[pl.BlockSpec(memory_space=pl.ANY)] * 6,
+        out_specs=pl.BlockSpec(memory_space=pl.ANY),
         scratch_shapes=scratch,
         compiler_params=pltpu.CompilerParams(collective_id=0, has_side_effects=True, vmem_limit_bytes=60 * 2**20),
         name="diloco",
-    )(*(a.T for a in (activations, out_grad, master_weights, first_moment, second_moment, anchor, outer_momentum)))
-    return rebuilt.T, momentum.T
+    )(*(a.T for a in operands)).T
+    new_momentum = NESTEROV * outer_momentum + pseudo_mean
+    rebuilt = anchor - OUTER_RATE * (pseudo_mean + NESTEROV * new_momentum)
+    return rebuilt.astype(jnp.bfloat16), new_momentum
 
 
 def solution(mesh):

time: 97.6 us -> 96.6 us (0.990)
  local copies, waits for them, and re-layouts: 3.36 us -> 0.01 us
  other arithmetic: 0 us -> 3.21 us
    unnamed x4, local copies, waits for them, and re-layouts: 3.36 us -> 0.01 us
    convert_element_type x0 -> x1, other arithmetic: none -> 3.21 us  [on_device(): return (rebuilt.astype(jnp.bfloat16), new_momentum)]
where the time goes in v3:
time: 96.6 us; the launch traced here: 96.5 us
  Pallas kernels  92.6 us (96%)
  other arithmetic  3.21 us (3%)
    pallas_call x1, Pallas kernels, on_device(): pl.pallas_call(kernel, out_shape=jax.ShapeDtypeStruct((hidden, features),...  92.6 us
    convert_element_type x1, other arithmetic, on_device(): return (rebuilt.astype(jnp.bfloat16), new_momentum)  3.21 us

profile of v3, /device:TPU:1, one launch (start us, length us, event | category | flops | bytes accessed | tf_op | source)
XLA Modules:
  0.0 96.5 jit_solution(15235413503104339699)
XLA Ops:
  0.6 0.0 copy-start
  0.6 0.0 copy-start.1
  0.7 92.6 %diloco.1 = f32[448,832]{1,0:T(8,128)} custom-call(bf16[832,256]{1,0:T(8,128)(2,1)} %bitcast.21, bf16[448,8192]{1,0:T(8,128)(2,1)} %bitcast.16, f32[448,832]{1,0:T(8,128)} %bitcast.18, f32[448,832]{1,0:T(8,128)} %bitcast.19, f32[448,832]{1,0:T(8,128)} %bitcast.20, f32[448,832]{1,0:T(8,128)} %bitcast.17), custom_call_target="tpu_custom_call" | custom-call | tf_op jit(solution)/shard_map/diloco/pallas_call | solution.py:454
  93.3 0.0 copy-done
  93.3 0.0 copy-done.1
  93.3 3.2 %fusion.2 = (bf16[832,448]{0,1:T(8,128)(2,1)}, f32[832,448]{0,1:T(8,128)}) fusion(f32[832,448]{0,1:T(8,128)S(1)} %copy-done, f32[448,832]{1,0:T(8,128)} %diloco.1, f32[832,448]{0,1:T(8,128)S(1)} %copy-done.1), kind=kLoop, calls=%fused_computation.4 | loop fusion | flops 2609152 | bytes 6709248 | tf_op jit(solution)/shard_map/convert_element_type | solution.py:465
Async XLA Ops:
  0.6 92.6 %copy-start = (f32[832,448]{0,1:T(8,128)S(1)}, f32[832,448]{0,1:T(8,128)}, u32[]{:S(2)}) copy-start(f32[832,448]{0,1:T(8,128)} %param.12) | copy-start | bytes 4472836
  0.6 92.6 %copy-start.1 = (f32[832,448]{0,1:T(8,128)S(1)}, f32[832,448]{0,1:T(8,128)}, u32[]{:S(2)}) copy-start(f32[832,448]{0,1:T(8,128)} %param.13) | copy-start | bytes 4472836

commit v4 on v3

--- a/solution.py
+++ b/solution.py
@@ -21,11 +21,11 @@
 NX, NZ, NC = 4, 4, 2
 RING = (0, -1, 1, 2)
 
-PHASES = ((256, "z"), (128, "x"), (256, "z"), (128, "z"), (64, "z"))
-MODES = ("yz", "yz", "yz", "yz", "all")
-RATE = {"x": 44e3, "z": 22e3, "d": 300e3, "y": 75e3}
-DELAY = {"x": 2.0, "z": 2.7, "d": 1.0, "y": 2.5}
-LEAD, BACKLOG = 1, 1.0
+PHASES = ((128, 'z'), (128, 'z'), (128, 'z'), (128, 'z'), (128, 'z'), (128, 'z'), (64, 'z'))
+MODES = ('yz', 'yz', 'yz', 'yz', 'yz', 'all', 'all')
+RATE = {'x': 47000.0, 'z': 15400.0, 'd': 278000.0, 'y': 62000.0}
+DELAY = {'x': 2.75, 'z': 3.98, 'd': 2.2, 'y': 2.78}
+LEAD, BACKLOG, RELAY = 0.5, 0.75, -0.3
 TILE_US, UPDATE_US, SEND_US = 3.5, 4.0, 0.02
 OTHER = {"x": "z", "z": "x"}
 
@@ -92,7 +92,7 @@
 
     def urgency(name):
         stage, p = name[:2]
-        return p - LEAD * (stage < 3) - 0.25 * (stage in (2, 4)), stage != 3 or name[3] != 2
+        return p - LEAD * (stage < 3) - RELAY * (stage in (2, 4)), stage != 3 or name[3] != 2
 
     def request(names):
         for name in names:

time: 96.6 us -> 95.7 us (level)
  no operation moved by 1% of the time
where the time goes in v4:
time: 95.7 us; the launch traced here: 95.6 us
  Pallas kernels  91.7 us (96%)
  other arithmetic  3.21 us (3%)
    pallas_call x1, Pallas kernels, on_device(): pl.pallas_call(kernel, out_shape=jax.ShapeDtypeStruct((hidden, features),...  91.7 us
    convert_element_type x1, other arithmetic, on_device(): return (rebuilt.astype(jnp.bfloat16), new_momentum)  3.21 us

profile of v4, /device:TPU:1, one launch (start us, length us, event | category | flops | bytes accessed | tf_op | source)
XLA Modules:
  0.0 95.6 jit_solution(7819261003633469083)
XLA Ops:
  0.6 0.0 copy-start
  0.6 0.0 copy-start.1
  0.7 91.7 %diloco.1 = f32[448,832]{1,0:T(8,128)} custom-call(bf16[832,256]{1,0:T(8,128)(2,1)} %bitcast.21, bf16[448,8192]{1,0:T(8,128)(2,1)} %bitcast.16, f32[448,832]{1,0:T(8,128)} %bitcast.18, f32[448,832]{1,0:T(8,128)} %bitcast.19, f32[448,832]{1,0:T(8,128)} %bitcast.20, f32[448,832]{1,0:T(8,128)} %bitcast.17), custom_call_target="tpu_custom_call" | custom-call | tf_op jit(solution)/shard_map/diloco/pallas_call | solution.py:454
  92.4 0.0 copy-done
  92.4 0.0 copy-done.1
  92.4 3.2 %fusion.2 = (bf16[832,448]{0,1:T(8,128)(2,1)}, f32[832,448]{0,1:T(8,128)}) fusion(f32[832,448]{0,1:T(8,128)S(1)} %copy-done, f32[448,832]{1,0:T(8,128)} %diloco.1, f32[832,448]{0,1:T(8,128)S(1)} %copy-done.1), kind=kLoop, calls=%fused_computation.4 | loop fusion | flops 2609152 | bytes 6709248 | tf_op jit(solution)/shard_map/convert_element_type | solution.py:465
Async XLA Ops:
  0.6 91.7 %copy-start = (f32[832,448]{0,1:T(8,128)S(1)}, f32[832,448]{0,1:T(8,128)}, u32[]{:S(2)}) copy-start(f32[832,448]{0,1:T(8,128)} %param.12) | copy-start | bytes 4472836
  0.6 91.7 %copy-start.1 = (f32[832,448]{0,1:T(8,128)S(1)}, f32[832,448]{0,1:T(8,128)}, u32[]{:S(2)}) copy-start(f32[832,448]{0,1:T(8,128)} %param.13) | copy-start | bytes 4472836
